TPU v7x, 128 devices: a whole 4x4x4 slice. The times are simulated.
128 devices in a mesh: rows: 16 (over y, x), cols: 8 (over z, core).
Axes of the slice: x: 4, y: 4, z: 4, core: 2. Of those that a mesh axis runs over, the one named last changes fastest.
Arguments:
- ensemble: bfloat16 [64, 768, 1024], P(None, 'rows', 'cols'), may hold values from -6 to 6
- row_profile: bfloat16 [768, 16384], P('rows'), may hold values from 0.0072021484 to 0.071777344
- col_profile: bfloat16 [1024, 16384], P('cols'), may hold values from 0.006225586 to 0.0625
- obs_owned: float32 [128, 384], P(('rows', 'cols')), may hold values from -18 to 18
- noise_owned: float32 [128, 384], P(('rows', 'cols')), may hold values from 40.96 to 409.6
- block_owner: int32 [128], replicated, may hold values from 0 to 127, as said below
Outputs:
- updated: bfloat16 [64, 768, 1024], P(None, 'rows', 'cols')
Inputs may be any that keep to these rules, and one draw needn't show every extreme that they name: `block_owner`: each of the 128 devices owns at most 3 detector blocks, and some devices own exactly 3, some own 1 and some own none.
All inputs are finite; a program needn't handle non-finite values.
Results may differ from a plain program's by a relative error of at most 0.0011.
Values sent between devices are 32-bit elements; how exact they have to be, the bound alone decides.
A program may use at most 128 MiB of HBM per device.

v0:
```python
import math

import jax
import jax.numpy as jnp
from jax import lax
from jax.sharding import PartitionSpec as P

MEMBERS = 64
BLOCK = 128
CAP = 3


def partial_blocks(flat_field, row_prof, col_prof, first_block, block_count):
    group_size = math.gcd(block_count, 8)
    group_count = block_count // group_size
    span_cols = group_size * BLOCK
    local_rows = row_prof.shape[0]

    def group_terms(step_at):
        first_col = (first_block + step_at * group_size) * BLOCK
        col_part = lax.dynamic_slice_in_dim(col_prof, first_col, span_cols, 1)
        row_part = lax.dynamic_slice_in_dim(row_prof, first_col, span_cols, 1).astype(jnp.float32)
        along_cols = jnp.dot(flat_field, col_part, preferred_element_type=jnp.float32)
        along_cols = along_cols.reshape(MEMBERS, local_rows, span_cols)
        summed = jnp.sum(along_cols * row_part[None], axis=1)
        return summed.reshape(MEMBERS, group_size, BLOCK).transpose(1, 0, 2)

    terms = lax.map(group_terms, jnp.arange(group_count, dtype=jnp.int32))
    return terms.reshape(block_count, MEMBERS, BLOCK)


def member_stats(predictions, observed, weights):
    member_mean = jnp.mean(predictions, axis=1, keepdims=True)
    anomalies = (predictions - member_mean) / math.sqrt(MEMBERS - 1)
    residuals = observed[:, None, :] - predictions
    scaled = anomalies * weights[:, None, :]
    spread_mat = jnp.einsum("sjd,skd->jk", scaled, anomalies, precision=lax.Precision.HIGHEST)
    innovation = jnp.einsum("sjd,skd->jk", scaled, residuals, precision=lax.Precision.HIGHEST)
    return (spread_mat, innovation)


def on_device(ensemble, row_profile, col_profile, obs_owned, noise_owned, block_owner):
    own_index = lax.axis_index(("rows", "cols"))
    devices = lax.axis_size(("rows", "cols"))
    blocks = col_profile.shape[1] // BLOCK
    local_rows = ensemble.shape[1]
    local_cols = ensemble.shape[2]
    flat_field = ensemble.reshape(MEMBERS * local_rows, local_cols)
    block_index = jnp.arange(blocks, dtype=jnp.int32)
    same_owner = block_owner[None, :] == block_owner[:, None]
    earlier = block_index[None, :] < block_index[:, None]
    slot_rank = jnp.sum((same_owner & earlier).astype(jnp.int32), axis=1)
    obs_slots = obs_owned.reshape(CAP, BLOCK)
    noise_slots = noise_owned.reshape(CAP, BLOCK)
    partials = partial_blocks(flat_field, row_profile, col_profile, 0, blocks)
    owner_grid = jnp.arange(devices, dtype=jnp.int32)[:, None, None]
    slot_grid = jnp.arange(CAP, dtype=jnp.int32)[None, :, None]
    slot_hit = (block_owner[None, None, :] == owner_grid) & (slot_rank[None, None, :] == slot_grid)
    slot_valid = jnp.any(slot_hit, axis=2)
    slot_block = jnp.sum(jnp.where(slot_hit, block_index[None, None, :], 0), axis=2)
    send_buffer = jnp.where(slot_valid[:, :, None, None], partials[slot_block], 0.0)
    predictions = jnp.sum(
        lax.all_to_all(send_buffer, ("rows", "cols"), split_axis=0, concat_axis=0, tiled=True),
        axis=0,
    )
    owned_count = jnp.sum((block_owner == own_index).astype(jnp.int32))
    live_slot = jnp.arange(CAP, dtype=jnp.int32) < owned_count
    weights = jnp.where(live_slot[:, None], 1.0 / noise_slots, 0.0)
    spread_mat, innovation = member_stats(predictions, obs_slots, weights)
    spread_mat, innovation = lax.psum((spread_mat, innovation), ("rows", "cols"))
    eye_mat = jnp.eye(MEMBERS, dtype=jnp.float32)
    factor = jnp.linalg.cholesky(eye_mat + spread_mat)
    gain_weights = jax.scipy.linalg.cho_solve((factor, True), innovation)
    field_flat = ensemble.astype(jnp.float32).reshape(MEMBERS, -1)
    member_mean = jnp.mean(field_flat, axis=0, keepdims=True)
    anomalies = (field_flat - member_mean) / math.sqrt(MEMBERS - 1)
    moved = field_flat + jnp.dot(gain_weights.T, anomalies, precision=lax.Precision.HIGHEST)
    return moved.reshape(ensemble.shape).astype(jnp.bfloat16)


def solution(mesh):
    in_specs = (
        P(None, "rows", "cols"),
        P("rows", None),
        P("cols", None),
        P(("rows", "cols"), None),
        P(("rows", "cols"), None),
        P(),
    )
    out_specs = P(None, "rows", "cols")
    return jax.shard_map(
        on_device, mesh=mesh, in_specs=in_specs, out_specs=out_specs, check_vma=False
    )
```

profile of v0, /device:TPU:1, one launch (start us, length us, event | category | flops | bytes accessed | tf_op | source)
XLA Modules:
  0.0 768.0 jit_solution(12466156515473649168)
XLA Ops:
  1.9 479.6 %while.12 = (s32[]{:T(128)}, f32[16,8,64,128]{3,2,1,0:T(8,128)}, s32[16]{0:T(128)S(1)}, bf16[128,16384]{1,0:T(8,128)(2,1)}, bf16[3072,128]{1,0:T(8,128)(2,1)}, /...) while((s32[]{:T(128)}, f32[16,8,64,128]{3,2,1,0:T(8,128)}, ...), condition=%wide.region_4.5_spmd, body=%wide.region_2.4_spmd.sunk | while | flops 811581440 | bytes 53182640 | solution.py:28
  3.3 7.6 convolution_bitcast_fusion.4
  10.9 12.6 %copy.39 = f32[3072,1024]{1,0:T(8,128)} copy(f32[3072,1024]{0,1:T(8,128)} %convolution_bitcast_fusion.4) | data formatting | bytes 25165824 | tf_op jit(solution)/shard_map/while/body/eval_jaxpr/dot_general | solution.py:23
  40.9 12.6 %copy.39 = f32[3072,1024]{1,0:T(8,128)} copy(f32[3072,1024]{0,1:T(8,128)} %convolution_bitcast_fusion.4) | data formatting | bytes 25165824 | tf_op jit(solution)/shard_map/while/body/eval_jaxpr/dot_general | solution.py:23
  63.2 7.6 convolution_bitcast_fusion.4
  70.8 12.6 %copy.39 = f32[3072,1024]{1,0:T(8,128)} copy(f32[3072,1024]{0,1:T(8,128)} %convolution_bitcast_fusion.4) | data formatting | bytes 25165824 | tf_op jit(solution)/shard_map/while/body/eval_jaxpr/dot_general | solution.py:23
  93.2 7.6 convolution_bitcast_fusion.4
  100.8 12.6 %copy.39 = f32[3072,1024]{1,0:T(8,128)} copy(f32[3072,1024]{0,1:T(8,128)} %convolution_bitcast_fusion.4) | data formatting | bytes 25165824 | tf_op jit(solution)/shard_map/while/body/eval_jaxpr/dot_general | solution.py:23
  130.8 12.6 %copy.39 = f32[3072,1024]{1,0:T(8,128)} copy(f32[3072,1024]{0,1:T(8,128)} %convolution_bitcast_fusion.4) | data formatting | bytes 25165824 | tf_op jit(solution)/shard_map/while/body/eval_jaxpr/dot_general | solution.py:23
  153.2 7.6 convolution_bitcast_fusion.4
  160.8 12.6 %copy.39 = f32[3072,1024]{1,0:T(8,128)} copy(f32[3072,1024]{0,1:T(8,128)} %convolution_bitcast_fusion.4) | data formatting | bytes 25165824 | tf_op jit(solution)/shard_map/while/body/eval_jaxpr/dot_general | solution.py:23
  183.1 7.6 convolution_bitcast_fusion.4
  190.8 12.6 %copy.39 = f32[3072,1024]{1,0:T(8,128)} copy(f32[3072,1024]{0,1:T(8,128)} %convolution_bitcast_fusion.4) | data formatting | bytes 25165824 | tf_op jit(solution)/shard_map/while/body/eval_jaxpr/dot_general | solution.py:23
  213.1 7.6 convolution_bitcast_fusion.4
  220.7 12.6 %copy.39 = f32[3072,1024]{1,0:T(8,128)} copy(f32[3072,1024]{0,1:T(8,128)} %convolution_bitcast_fusion.4) | data formatting | bytes 25165824 | tf_op jit(solution)/shard_map/while/body/eval_jaxpr/dot_general | solution.py:23
  243.1 7.6 convolution_bitcast_fusion.4
  250.7 12.6 %copy.39 = f32[3072,1024]{1,0:T(8,128)} copy(f32[3072,1024]{0,1:T(8,128)} %convolution_bitcast_fusion.4) | data formatting | bytes 25165824 | tf_op jit(solution)/shard_map/while/body/eval_jaxpr/dot_general | solution.py:23
  273.1 7.6 convolution_bitcast_fusion.4
  280.7 12.6 %copy.39 = f32[3072,1024]{1,0:T(8,128)} copy(f32[3072,1024]{0,1:T(8,128)} %convolution_bitcast_fusion.4) | data formatting | bytes 25165824 | tf_op jit(solution)/shard_map/while/body/eval_jaxpr/dot_general | solution.py:23
  310.7 12.6 %copy.39 = f32[3072,1024]{1,0:T(8,128)} copy(f32[3072,1024]{0,1:T(8,128)} %convolution_bitcast_fusion.4) | data formatting | bytes 25165824 | tf_op jit(solution)/shard_map/while/body/eval_jaxpr/dot_general | solution.py:23
  340.6 12.6 %copy.39 = f32[3072,1024]{1,0:T(8,128)} copy(f32[3072,1024]{0,1:T(8,128)} %convolution_bitcast_fusion.4) | data formatting | bytes 25165824 | tf_op jit(solution)/shard_map/while/body/eval_jaxpr/dot_general | solution.py:23
  370.6 12.6 %copy.39 = f32[3072,1024]{1,0:T(8,128)} copy(f32[3072,1024]{0,1:T(8,128)} %convolution_bitcast_fusion.4) | data formatting | bytes 25165824 | tf_op jit(solution)/shard_map/while/body/eval_jaxpr/dot_general | solution.py:23
  392.9 7.6 convolution_bitcast_fusion.4
  400.6 12.6 %copy.39 = f32[3072,1024]{1,0:T(8,128)} copy(f32[3072,1024]{0,1:T(8,128)} %convolution_bitcast_fusion.4) | data formatting | bytes 25165824 | tf_op jit(solution)/shard_map/while/body/eval_jaxpr/dot_general | solution.py:23
  430.5 12.6 %copy.39 = f32[3072,1024]{1,0:T(8,128)} copy(f32[3072,1024]{0,1:T(8,128)} %convolution_bitcast_fusion.4) | data formatting | bytes 25165824 | tf_op jit(solution)/shard_map/while/body/eval_jaxpr/dot_general | solution.py:23
  452.9 7.6 convolution_bitcast_fusion.4
  460.5 12.6 %copy.39 = f32[3072,1024]{1,0:T(8,128)} copy(f32[3072,1024]{0,1:T(8,128)} %convolution_bitcast_fusion.4) | data formatting | bytes 25165824 | tf_op jit(solution)/shard_map/while/body/eval_jaxpr/dot_general | solution.py:23
  482.0 8.1 %gather_fusion = f32[384,64,128]{2,1,0:T(8,128)} fusion(f32[128,64,128]{2,1,0:T(8,128)} %bitcast.75, s32[1024]{0:T(1024)S(1)} %pad_clamp_fusion), kind=kCustom, calls=%fused_computation | custom fusion | bytes 25167360 | tf_op jit(solution)/shard_map/gather | solution.py:61
  490.1 10.2 %broadcast_select_fusion = f32[128,3,64,128]{3,2,1,0:T(8,128)} fusion(f32[128,3,64,128]{3,2,1,0:T(8,128)} %bitcast.71, pred[128,3]{1,0:T(8,128)(4,1)S(1)} %copy.15), kind=kLoop, calls=%fused_computation.9 | loop fusion | flops 3145728 | bytes 25166208 | tf_op jit(solution)/shard_map/jit(_where)/select_n | solution.py:61
  500.3 11.9 %all-to-all-start = ((f32[128,3,64,128]{3,2,1,0:T(8,128)}), f32[128,3,64,128]{3,2,1,0:T(8,128)}, u32[]{:S(2)}, u32[]{:S(2)}) async-start(f32[128,3,64,128]{3,2,1,0:T(8,128)} %broadcast_select_fusion), calls=%async_computation | async-start | bytes 25165824 | tf_op jit(solution)/shard_map/all_to_all | solution.py:63
  514.0 160.1 %all-to-all-done = f32[128,3,64,128]{3,2,1,0:T(8,128)} async-done(((f32[128,3,64,128]{3,2,1,0:T(8,128)}), f32[128,3,64,128]{3,2,1,0:T(8,128)}, u32[]{:S(2)}, u32[]{:S(2)}) %all-to-all-start) | async-done | bytes 12582944 | tf_op jit(solution)/shard_map/all_to_all | solution.py:63
  681.0 70.9 %all-reduce = (f32[64,64]{1,0:T(8,128)S(1)}, f32[64,64]{1,0:T(8,128)S(1)}) all-reduce(f32[64,64]{1,0:T(8,128)S(1)} %convolution_bitcast_fusion.1, f32[64,64]{1,0:T(8,128)S(1)} %convolution_bitcast_fusion.2), channel_id=1, replica_groups=mesh['rows'=16,'cols'=8] {'rows','cols'}, use_global_device_ids=true, to_apply=%region_12.13 | all-reduce | flops 8192 | bytes 65536 | tf_op jit(solution)/shard_map/psum | solution.py:70
  (130 shorter events, 217.1 us)
Async XLA Ops:
  500.3 11.9 %copy-start = (bf16[3072,128]{1,0:T(8,128)(2,1)S(1)}, bf16[3072,128]{1,0:T(8,128)(2,1)}, u32[]{:S(2)}) copy-start(bf16[3072,128]{1,0:T(8,128)(2,1)} %get-tuple-element.174) | copy-start | bytes 2359300
  500.3 12.1 %copy-start.2 = (f32[1,384]{1,0:T(1,128)S(1)}, f32[1,384]{1,0:T(1,128)}, u32[]{:S(2)}) copy-start(f32[1,384]{1,0:T(1,128)} %param.11) | copy-start | bytes 4612
  500.3 12.1 %copy-start.3 = (s32[128]{0:T(128)S(1)}, s32[128]{0:T(128)}, u32[]{:S(2)}) copy-start(s32[128]{0:T(128)} %param.13) | copy-start | bytes 1540
  500.3 13.4 %copy-start.1 = (f32[1,384]{1,0:T(1,128)S(1)}, f32[1,384]{1,0:T(1,128)}, u32[]{:S(2)}) copy-start(f32[1,384]{1,0:T(1,128)} %param.12) | copy-start | bytes 4612
  500.3 173.8 %all-to-all-start = ((f32[128,3,64,128]{3,2,1,0:T(8,128)}), f32[128,3,64,128]{3,2,1,0:T(8,128)}, u32[]{:S(2)}, u32[]{:S(2)}) async-start(f32[128,3,64,128]{3,2,1,0:T(8,128)} %broadcast_select_fusion), calls=%async_computation | async-start | bytes 25165824 | tf_op jit(solution)/shard_map/all_to_all | solution.py:63
where the time goes:
time: 772 us; the launch traced here: 768 us
  local copies, waits for them, and re-layouts  235 us (30%)
  waiting for transfers between devices  160 us (21%)
  other arithmetic  153 us (20%)
  matrix products  125 us (16%)
  blocking collectives  70.9 us (9%)
  starting transfers between devices  11.9 us (2%)
  loops' own time  11.5 us (1%)
    dot_general x16, local copies, waits for them, and re-layouts, group_terms(): jnp.dot(flat_field, col_part, preferred_element_type=jnp.float32)  201 us
    all_to_all x1, waiting for transfers between devices, on_device(): lax.all_to_all(send_buffer, ('rows', 'cols'), split_axis=0, concat_axis=0...  160 us
    dot_general x16, matrix products, group_terms(): jnp.dot(flat_field, col_part, preferred_element_type=jnp.float32)  122 us
    reduce_sum x16, other arithmetic, group_terms(): summed = jnp.sum(along_cols * row_part[None], axis=1)  106 us
    psum x1, blocking collectives, on_device(): lax.psum((spread_mat, innovation), ('rows', 'cols'))  70.9 us
  transfers between devices with their start and end apart: 1, of which 1 were waited for; matrix products, arithmetic and copies ran while one was open for 0% of the time, Pallas kernels for 0%

commit v1 on v0

v1 whole, which is shorter than its diff:
```python
import functools
import math

import jax
import jax.numpy as jnp
from jax import lax
from jax.experimental import pallas as pl
from jax.experimental.pallas import tpu as pltpu
from jax.sharding import PartitionSpec as P

MEMBERS = 64
BLOCK = 128
CAP = 3
LROWS = 48
LCOLS = 128
STEPS = 16
WIDE = 512
AHEAD = 3
LAG2 = 3
LAG3 = 6
ROOT = math.sqrt(MEMBERS - 1)
MESH = pl.DeviceIdType.MESH
F32 = jnp.float32
BF16 = jnp.bfloat16


def here():
    r = lax.axis_index("rows")
    c = lax.axis_index("cols")
    return r // 4, r % 4, c // 2, c % 2


def device(y, x, z, k):
    return (y * 4 + x, z * 2 + k)


def partial_kernel(
    e_hbm, col_hbm, row_hbm, obs_ref, noise_ref, owner_ref,
    sums_ref, et_hbm,
    e_v, ef, esend, erecv, lhs, col_v, row_v, csend, crecv, rhs, rowf, pa, pb, pc,
    ra1, ra2, ra3, rb1, rb2, rb3, rc1, rc2, rc3, slots, pack, got_core, got,
    e_sem, et_sem, col_sem, row_sem,
    es_sem, er_sem, cs_sem, cr_sem,
    sa, sb, sc,
    qa1, qa2, qa3, qb1, qb2, qb3, qc1, qc2, qc3,
    so, qo_z, qo_x, qo_y, qo_k,
    st, qt,
):
    y, x, z, k = here()
    sibling = device(y, x, z, 1 - k)

    def zpeer(d):
        return device(y, x, (z + d) % 4, k)

    def xpeer(d):
        return device(y, (x + d) % 4, z, k)

    def ypeer(d):
        return device((y + d) % 4, x, z, k)

    def remote(src, dst, send, recv, to):
        return pltpu.make_async_remote_copy(
            src_ref=src, dst_ref=dst, send_sem=send, recv_sem=recv,
            device_id=to, device_id_type=MESH,
        )

    def sent(src, sem):
        remote(src, src, sem, sem, sibling).wait_send()

    def landed(dst, sem):
        remote(dst, dst, sem, sem, sibling).wait_recv()

    def span(core, s):
        dz, dx = 3 - s // 4, 3 - s % 4
        first = ((core * 4 + (z + dz) % 4) * 4 + (x + dx) % 4) * WIDE
        return pl.ds(pl.multiple_of(first, WIDE), WIDE)

    def load_col(which, s):
        core = k if which == 0 else 1 - k
        return pltpu.make_async_copy(
            col_hbm.at[:, span(core, s)], col_v.at[which, s], col_sem.at[which, s]
        )

    def load_row(s):
        return pltpu.make_async_copy(
            row_hbm.at[:, span(k, s)], row_v.at[s], row_sem.at[s]
        )

    load_e = pltpu.make_async_copy(e_hbm, e_v, e_sem)
    load_e.start()

    barrier = pltpu.get_barrier_semaphore()
    pl.semaphore_signal(barrier, 1, device_id=sibling, device_id_type=MESH)
    for d in (1, 2, 3):
        for peer in (zpeer(d), xpeer(d), ypeer(d)):
            pl.semaphore_signal(barrier, 1, device_id=peer, device_id_type=MESH)

    def start_loads(s, carry):
        load_col(1, s).start()
        load_col(0, s).start()
        load_row(s).start()
        return carry

    lax.fori_loop(0, STEPS, start_loads, 0)

    home = k * 64 + (y * 4 + x) * 4 + z
    pack[...] = jnp.zeros_like(pack)
    for i in range(CAP):
        pack[i:i + 1, :] = obs_ref[:, i * BLOCK:(i + 1) * BLOCK]
        pack[4 + i:5 + i, :] = noise_ref[:, i * BLOCK:(i + 1) * BLOCK]
    slots[home] = pack[...]

    load_e.wait()
    ef[...] = e_v[...].astype(F32)

    pl.semaphore_wait(barrier, 10)

    quarter = MEMBERS * LROWS // 4
    for piece in range(4):
        for i in range(12):
            at = piece * 12 + i
            plane = ef[pl.ds(at, MEMBERS, stride=LROWS), :]
            esend[at * MEMBERS:(at + 1) * MEMBERS, :] = plane
            lhs[at * MEMBERS:(at + 1) * MEMBERS, 0:LCOLS] = plane.astype(BF16)
        part_rows = pl.ds(piece * quarter, quarter)
        remote(
            esend.at[part_rows], erecv.at[part_rows], es_sem, er_sem.at[piece], sibling
        ).start()

    def send_col(s):
        load_col(1, s).wait()
        csend[s] = col_v[1, s].astype(F32)
        remote(csend.at[s], crecv.at[s], cs_sem, cr_sem.at[s], sibling).start()

    for s in range(AHEAD):
        send_col(s)

    for d in (1, 2, 3):
        remote(slots.at[home], slots.at[home], so, qo_z.at[d - 1], zpeer(d)).start()

    for piece in range(4):
        part_rows = pl.ds(piece * quarter, quarter)
        landed(erecv.at[part_rows], er_sem.at[piece])
        lhs[piece * quarter:(piece + 1) * quarter, LCOLS:2 * LCOLS] = (
            erecv[piece * quarter:(piece + 1) * quarter, :].astype(BF16)
        )
    save_et = pltpu.make_async_copy(lhs.at[:, pl.ds(0, LCOLS)], et_hbm, et_sem)
    save_et.start()

    def compute(s):
        load_col(0, s).wait()
        load_row(s).wait()
        landed(crecv.at[s], cr_sem.at[s])
        rhs[0:LCOLS, :] = col_v[0, s]
        rhs[LCOLS:2 * LCOLS, :] = crecv[s].astype(BF16)
        rowf[...] = row_v[s].astype(F32)
        total = jnp.zeros((MEMBERS, WIDE), F32)
        group = 4
        for g in range(LROWS // group):
            rows = group * MEMBERS
            along = jnp.dot(
                lhs[g * rows:(g + 1) * rows, :], rhs[...], preferred_element_type=F32
            )
            for i in range(group):
                at = g * group + i
                total += along[i * MEMBERS:(i + 1) * MEMBERS] * rowf[at:at + 1, :]
        for q in range(4):
            lanes = slice(q * BLOCK, (q + 1) * BLOCK)
            turn = (q - y + 4) % 4
            pa[s, turn] = total[0:24, lanes]
            pb[s, turn] = total[24:48, lanes]
            pc[s, turn] = total[48:64, lanes]

    def first_sends(w, j):
        s, dz, dx = 4 * w + j, 3 - w, 3 - j

        @pl.when(dz != 0)
        def _():
            remote(
                pa.at[s], ra1.at[dz - 1, j],
                sa.at[0], qa1.at[dz - 1, j], zpeer(dz),
            ).start()

        if dx != 0:
            remote(
                pb.at[s], rb1.at[w, dx - 1],
                sb.at[0], qb1.at[w, dx - 1], xpeer(dx),
            ).start()

        for d in (1, 2, 3):
            remote(
                pc.at[s, d], rc1.at[s, d - 1],
                sc.at[0], qc1.at[s, d - 1], ypeer(d),
            ).start()

    def second_a(w, j):
        s, dz, dx = 4 * w + j, 3 - w, 3 - j

        @pl.when(dz == 0)
        def _():
            for p in range(3):
                landed(ra1.at[p, j], qa1.at[p, j])
            pa[s] = pa[s] + (
                ra1[0, j] + (ra1[1, j] + ra1[2, j])
            )

            if dx != 0:
                remote(
                    pa.at[s], ra2.at[dx - 1],
                    sa.at[1], qa2.at[dx - 1], xpeer(dx),
                ).start()

    def second_b(w, j):
        s, dz, dx = 4 * w + j, 3 - w, 3 - j

        if dx == 0:
            for p in range(3):
                landed(rb1.at[w, p], qb1.at[w, p])
            pb[s] = pb[s] + (rb1[w, 0] + (rb1[w, 1] + rb1[w, 2]))
            for d in (1, 2, 3):
                remote(
                    pb.at[s, d], rb2.at[w, d - 1],
                    sb.at[1], qb2.at[w, d - 1], ypeer(d),
                ).start()

    def second_c(w, j):
        s, dz, dx = 4 * w + j, 3 - w, 3 - j
        for p in range(3):
            landed(rc1.at[s, p], qc1.at[s, p])
        pc[s, 0] = pc[s, 0] + (rc1[s, 0] + (rc1[s, 1] + rc1[s, 2]))

        @pl.when(dz != 0)
        def _():
            remote(
                pc.at[s, 0], rc2.at[dz - 1, j],
                sc.at[1], qc2.at[dz - 1, j], zpeer(dz),
            ).start()

    def third_a():
        s = STEPS - 1
        for p in range(3):
            landed(ra2.at[p], qa2.at[p])
        pa[s] = pa[s] + (ra2[0] + (ra2[1] + ra2[2]))
        for d in (1, 2, 3):
            remote(
                pa.at[s, d], ra3.at[d - 1],
                sa.at[2], qa3.at[d - 1], ypeer(d),
            ).start()

    def third_b(w, j):
        s, dz, dx = 4 * w + j, 3 - w, 3 - j

        if dx == 0:
            for p in range(3):
                landed(rb2.at[w, p], qb2.at[w, p])
            pb[s, 0] = pb[s, 0] + (rb2[w, 0] + (rb2[w, 1] + rb2[w, 2]))

            @pl.when(dz != 0)
            def _():
                remote(
                    pb.at[s, 0], rb3.at[dz - 1],
                    sb.at[2], qb3.at[dz - 1], zpeer(dz),
                ).start()

    def third_c(w, j):
        s, dz, dx = 4 * w + j, 3 - w, 3 - j

        @pl.when(dz == 0)
        def _():
            for p in range(3):
                landed(rc2.at[p, j], qc2.at[p, j])
            pc[s, 0] = pc[s, 0] + (
                rc2[0, j] + (rc2[1, j] + rc2[2, j])
            )

            if dx != 0:
                remote(
                    pc.at[s, 0], rc3.at[dx - 1],
                    sc.at[2], qc3.at[dx - 1], xpeer(dx),
                ).start()

    base_x = k * 64 + (y * 4 + x) * 4
    base_y = k * 64 + y * 16
    base_k = k * 64

    def slots_x():
        for d in (1, 2, 3):
            landed(slots.at[home], qo_z.at[d - 1])
        mine = slots.at[pl.ds(base_x, 4)]
        for d in (1, 2, 3):
            remote(mine, mine, so, qo_x.at[d - 1], xpeer(d)).start()

    def slots_y():
        for d in (1, 2, 3):
            landed(slots.at[pl.ds(base_x, 4)], qo_x.at[d - 1])
        mine = slots.at[pl.ds(base_y, 16)]
        for d in (1, 2, 3):
            remote(mine, mine, so, qo_y.at[d - 1], ypeer(d)).start()

    def slots_k():
        for d in (1, 2, 3):
            landed(slots.at[pl.ds(base_y, 16)], qo_y.at[d - 1])
        mine = slots.at[pl.ds(base_k, 64)]
        remote(mine, mine, so, qo_k, sibling).start()

    def lagged(events, w, j, lag):
        back = (j - lag) // 4
        late, at = w + back, (j - lag) % 4

        def run():
            for event in events:
                event(late, at)

        if back == 0:
            run()
        else:
            pl.when(late >= 0)(run)

    def phase(w, carry):
        for j in range(4):
            s = 4 * w + j
            pl.when(s + AHEAD < STEPS)(functools.partial(send_col, s + AHEAD))
            compute(s)
            first_sends(w, j)
            lagged((second_a, second_b, second_c), w, j, LAG2)
            lagged((third_b, third_c), w, j, LAG3)
        pl.when(w == 0)(slots_x)
        pl.when(w == 1)(slots_y)
        pl.when(w == 2)(slots_k)
        return carry

    lax.fori_loop(0, STEPS // 4, phase, 0)

    last = STEPS - 1
    for s in range(STEPS - LAG2, last):
        second_a(s // 4, s % 4)
        second_b(s // 4, s % 4)
        second_c(s // 4, s % 4)
    for s in range(STEPS - LAG3, last):
        third_b(s // 4, s % 4)
        third_c(s // 4, s % 4)
    second_a(3, 3)
    second_b(3, 3)
    third_a()
    second_c(3, 3)
    third_c(3, 3)
    third_b(3, 3)

    landed(slots.at[pl.ds(base_k, 64)], qo_k)
    me = ((k * 4 + z) * 4 + x) * 4 + y
    owner = owner_ref[me]

    def count(b, n):
        return n + jnp.where(jnp.logical_and(owner_ref[b] == owner, b < me), 1, 0)

    rank = lax.fori_loop(0, owner_ref.shape[0], count, jnp.int32(0))
    o_row, o_col = owner // 8, owner % 8
    found = slots[(o_col % 2) * 64 + o_row * 4 + o_col // 2]
    observed = jnp.where(
        rank == 0, found[0:1], jnp.where(rank == 1, found[1:2], found[2:3])
    )
    variance = jnp.where(
        rank == 0, found[4:5], jnp.where(rank == 1, found[5:6], found[6:7])
    )
    weight = 1.0 / variance

    for d in range(3):
        landed(ra3.at[d], qa3.at[d])
        landed(rb3.at[d], qb3.at[d])
        landed(rc3.at[d], qc3.at[d])
    predictions = jnp.concatenate(
        [
            pa[last, 0] + (ra3[0] + (ra3[1] + ra3[2])),
            pb[last, 0] + (rb3[0] + (rb3[1] + rb3[2])),
            pc[last, 0] + (rc3[0] + (rc3[1] + rc3[2])),
        ],
        axis=0,
    )
    mean = jnp.mean(predictions, axis=0, keepdims=True)
    anomalies = (predictions - mean) * (1.0 / ROOT)
    scaled = anomalies * weight
    offset = jnp.where(
        lax.broadcasted_iota(jnp.int32, (8, BLOCK), 0) == 0, observed - mean, 0.0
    )
    blank = jnp.zeros((8, BLOCK), F32)
    left = jnp.concatenate([anomalies[0:16], anomalies[32:48], offset], axis=0)
    right = jnp.concatenate([anomalies[16:32], anomalies[48:64], blank], axis=0)
    none = jnp.zeros((MEMBERS, BLOCK), F32)
    contract = (((1,), (1,)), ((), ()))
    packed = lax.dot_general(
        left, jnp.concatenate([scaled, none], axis=0), contract,
        precision=lax.Precision.HIGHEST, preferred_element_type=F32,
    ) + lax.dot_general(
        right, jnp.concatenate([none, scaled], axis=0), contract,
        precision=lax.Precision.HIGHEST, preferred_element_type=F32,
    )
    got[0, 0, 0:16] = packed[0:16]
    got[0, 0, 16:24] = packed[32:40]
    got[0, 1, 0:16] = packed[16:32]
    got[0, 1, 16:24] = jnp.zeros((8, BLOCK), F32)

    remote(got.at[0, 1 - k], got_core.at[0], st.at[0], qt.at[0], sibling).start()
    landed(got_core.at[0], qt.at[0])
    got[1, 0] = got[0, k] + got_core[0]
    for stage, peers in enumerate((zpeer, xpeer, ypeer)):
        for d in (1, 2, 3):
            remote(
                got.at[1 + stage, 0], got_core.at[1 + 3 * stage + d - 1],
                st.at[1 + 3 * stage + d - 1], qt.at[1 + 3 * stage + d - 1], peers(d),
            ).start()
        for d in (1, 2, 3):
            landed(got_core.at[1 + 3 * stage + d - 1], qt.at[1 + 3 * stage + d - 1])
        first = 1 + 3 * stage
        total = got[1 + stage, 0] + (
            got_core[first] + (got_core[first + 1] + got_core[first + 2])
        )
        got[2 + stage, 0] = total
    remote(got.at[4, 0], got_core.at[10], st.at[10], qt.at[10], sibling).start()
    sums_ref[k] = got[4, 0]
    landed(got_core.at[10], qt.at[10])
    sums_ref[1 - k] = got_core[10]

    save_et.wait()
    sent(esend, es_sem)
    sent(csend, cs_sem)
    sent(pa.at[pl.ds(0, 12), :], sa.at[0])
    sent(pa.at[pl.ds(0, 3), :], sa.at[1])
    sent(pa.at[0, pl.ds(0, 3)], sa.at[2])
    sent(pb.at[pl.ds(0, 12), :], sb.at[0])
    sent(pb.at[pl.ds(0, 4), pl.ds(0, 3)], sb.at[1])
    sent(pb.at[0, pl.ds(0, 3)], sb.at[2])
    sent(pc.at[pl.ds(0, 16), pl.ds(0, 3)], sc.at[0])
    sent(pc.at[pl.ds(0, 12), 0], sc.at[1])
    sent(pc.at[0, pl.ds(0, 3)], sc.at[2])
    sent(slots.at[pl.ds(0, 3 + 12 + 48 + 64)], so)
    for i in range(11):
        sent(got_core.at[0], st.at[i])


def apply_kernel(sums_ref, et_ref, out_ref, full):
    low = sums_ref[0, 0:16]
    high = sums_ref[1, 0:16]
    spread = jnp.concatenate(
        [low, pltpu.roll(low, 64, 1), high, pltpu.roll(high, 64, 1)], axis=0
    )
    r_row = sums_ref[0, 16:17] + sums_ref[1, 16:17]
    row_at = lax.broadcasted_iota(jnp.int32, (MEMBERS, 2 * MEMBERS), 0)
    lane_at = lax.broadcasted_iota(jnp.int32, (MEMBERS, 2 * MEMBERS), 1)
    left = lane_at < MEMBERS
    eye = jnp.where(row_at == lane_at, 1.0, 0.0)
    grid = jnp.where(left, spread + eye, jnp.where(lane_at - MEMBERS == row_at, 1.0, 0.0))
    for p in range(MEMBERS):
        pivot_row = grid[p:p + 1, :]
        scaled = pivot_row / pivot_row[:, p:p + 1]
        grid = jnp.where(row_at == p, scaled, grid - grid[:, p:p + 1] * scaled)
    inverse = jnp.where(left, pltpu.roll(grid, 64, 1), 0.0)
    r_col = jnp.sum(jnp.where(row_at == lane_at, r_row, 0.0), axis=1, keepdims=True)
    shift = jnp.sum(inverse * r_col, axis=0, keepdims=True)
    gain_t = jnp.where(left, shift - ROOT * (eye - inverse), 0.0)
    centre = jnp.sum(gain_t, axis=1, keepdims=True) * (1.0 / MEMBERS)
    moves = jnp.where(left, (gain_t - centre) * (1.0 / ROOT), 0.0)
    one = moves.astype(BF16).astype(F32)
    two = (moves - one).astype(BF16).astype(F32)
    three = moves - one - two
    factors = jnp.concatenate(
        [(one + pltpu.roll(two, 64, 1)).astype(BF16), three.astype(BF16)], axis=1
    )[:, 0:2 * BLOCK]
    zero = jnp.zeros((MEMBERS, 2 * BLOCK), BF16)
    for g in range(LROWS // 2):
        at = 2 * g * MEMBERS
        pair = jnp.concatenate(
            [et_ref[at:at + MEMBERS, :], et_ref[at + MEMBERS:at + 2 * MEMBERS, :]], axis=1
        )
        moved = pair.astype(F32) + jnp.dot(
            factors, jnp.concatenate([pair, pair, pair, zero], axis=0),
            preferred_element_type=F32,
        )
        full[pl.ds(2 * g, MEMBERS, stride=LROWS), :] = moved[:, 0:BLOCK]
        full[pl.ds(2 * g + 1, MEMBERS, stride=LROWS), :] = moved[:, BLOCK:2 * BLOCK]
    out_ref[...] = full[...].astype(BF16)


def on_device(ensemble, row_profile, col_profile, obs_owned, noise_owned, block_owner):
    field = ensemble.reshape(MEMBERS * LROWS, LCOLS)
    hbm = pl.BlockSpec(memory_space=pltpu.HBM)
    vmem = pl.BlockSpec(memory_space=pltpu.VMEM)
    smem = pl.BlockSpec(memory_space=pltpu.SMEM)
    dma = pltpu.SemaphoreType.DMA
    size = MEMBERS * LROWS
    sums, field_t = pl.pallas_call(
        partial_kernel,
        name="partial_sums",
        out_shape=(
            jax.ShapeDtypeStruct((2, 24, BLOCK), F32),
            jax.ShapeDtypeStruct((size, LCOLS), BF16),
        ),
        in_specs=[hbm, hbm, hbm, vmem, vmem, smem],
        out_specs=(vmem, hbm),
        scratch_shapes=[
            pltpu.VMEM((size, LCOLS), BF16),
            pltpu.VMEM((size, LCOLS), F32),
            pltpu.VMEM((size, LCOLS), F32),
            pltpu.VMEM((size, LCOLS), F32),
            pltpu.VMEM((size, 2 * LCOLS), BF16),
            pltpu.VMEM((2, STEPS, LCOLS, WIDE), BF16),
            pltpu.VMEM((STEPS, LROWS, WIDE), BF16),
            pltpu.VMEM((STEPS, LCOLS, WIDE), F32),
            pltpu.VMEM((STEPS, LCOLS, WIDE), F32),
            pltpu.VMEM((2 * LCOLS, WIDE), BF16),
            pltpu.VMEM((LROWS, WIDE), F32),
            pltpu.VMEM((STEPS, 4, 24, BLOCK), F32),
            pltpu.VMEM((STEPS, 4, 24, BLOCK), F32),
            pltpu.VMEM((STEPS, 4, 16, BLOCK), F32),
            pltpu.VMEM((3, 4, 4, 24, BLOCK), F32),
            pltpu.VMEM((3, 4, 24, BLOCK), F32),
            pltpu.VMEM((3, 24, BLOCK), F32),
            pltpu.VMEM((4, 3, 4, 24, BLOCK), F32),
            pltpu.VMEM((4, 3, 24, BLOCK), F32),
            pltpu.VMEM((3, 24, BLOCK), F32),
            pltpu.VMEM((STEPS, 3, 16, BLOCK), F32),
            pltpu.VMEM((3, 4, 16, BLOCK), F32),
            pltpu.VMEM((3, 16, BLOCK), F32),
            pltpu.VMEM((128, 8, BLOCK), F32),
            pltpu.VMEM((8, BLOCK), F32),
            pltpu.VMEM((11, 24, BLOCK), F32),
            pltpu.VMEM((5, 2, 24, BLOCK), F32),
            dma, dma, dma((2, STEPS)), dma((STEPS,)),
            dma, dma((4,)), dma, dma((STEPS,)),
            dma((3,)), dma((3,)), dma((3,)),
            dma((3, 4)), dma((3,)), dma((3,)),
            dma((4, 3)), dma((4, 3)), dma((3,)),
            dma((STEPS, 3)), dma((3, 4)), dma((3,)),
            dma, dma((3,)), dma((3,)), dma((3,)), dma,
            dma((11,)), dma((11,)),
        ],
        compiler_params=pltpu.CompilerParams(
            collective_id=0, has_side_effects=True, vmem_limit_bytes=48 << 20
        ),
    )(field, col_profile, row_profile, obs_owned, noise_owned, block_owner)
    moved = pl.pallas_call(
        apply_kernel,
        name="solve_apply",
        out_shape=jax.ShapeDtypeStruct((size, LCOLS), BF16),
        in_specs=[vmem, vmem],
        out_specs=vmem,
        scratch_shapes=[pltpu.VMEM((size, LCOLS), F32)],
        compiler_params=pltpu.CompilerParams(vmem_limit_bytes=32 << 20),
    )(sums, field_t)
    return moved.reshape(ensemble.shape)


def solution(mesh):
    in_specs = (
        P(None, "rows", "cols"),
        P("rows", None),
        P("cols", None),
        P(("rows", "cols"), None),
        P(("rows", "cols"), None),
        P(),
    )
    return jax.shard_map(
        on_device, mesh=mesh, in_specs=in_specs, out_specs=P(None, "rows", "cols"),
        check_vma=False,
    )
```

time: 772 us -> 66 us (0.09)
  local copies, waits for them, and re-layouts: 235 us -> 4.55 us
  waiting for transfers between devices: 160 us -> 0 us
  other arithmetic: 153 us -> 0 us
  matrix products: 125 us -> 0 us
  blocking collectives: 70.9 us -> 0 us
  Pallas kernels: 0 us -> 61.2 us
  starting transfers between devices: 11.9 us -> 0 us
  loops' own time: 11.5 us -> 0 us
    dot_general x16 -> x0, local copies, waits for them, and re-layouts: 201 us -> none  [group_terms(): jnp.dot(flat_field, col_part, preferred_element_type=jnp.float32)]
    all_to_all x1 -> x0, waiting for transfers between devices: 160 us -> none  [on_device(): lax.all_to_all(send_buffer, ('rows', 'cols'), split_axis=0, concat_axis=0...]
    dot_general x19 -> x0, matrix products: 125 us -> none  [the longest x16 122 us: group_terms(): jnp.dot(flat_field, col_part, preferred_element_type=jnp.float32)]
    reduce_sum x21 -> x0, other arithmetic: 115 us -> none  [the longest x16 106 us: group_terms(): summed = jnp.sum(along_cols * row_part[None], axis=1)]
    psum x1 -> x0, blocking collectives: 70.9 us -> none  [on_device(): lax.psum((spread_mat, innovation), ('rows', 'cols'))]
    pallas_call x0 -> x2, Pallas kernels: none -> 61.2 us  [the longest x1 53.9 us: on_device(): pl.pallas_call(partial_kernel, name='partial_sums', out_shape=(jax.ShapeD...]
    convert_element_type x16 -> x0, other arithmetic: 14.5 us -> none  [group_terms(): lax.dynamic_slice_in_dim(row_prof, first_col, span_cols, 1)]
    dynamic_update_slice x16 -> x0, local copies, waits for them, and re-layouts: 12.2 us -> none  [partial_blocks(): terms = lax.map(group_terms, jnp.arange(group_count, dtype=jnp.int32))]
  transfers between devices with their start and end apart: 1 -> 0, of which waited for: 1 -> 0; matrix products, arithmetic and copies ran while one was open for 0% -> 0% of each run, Pallas kernels for 0% -> 0%
where the time goes in v1:
time: 66 us; the launch traced here: 65.8 us
  Pallas kernels  61.2 us (93%)
  local copies, waits for them, and re-layouts  4.55 us (7%)
    pallas_call x1, Pallas kernels, on_device(): pl.pallas_call(partial_kernel, name='partial_sums', out_shape=(jax.ShapeD...  53.9 us
    pallas_call x1, Pallas kernels, on_device(): pl.pallas_call(apply_kernel, name='solve_apply', out_shape=jax.ShapeDtype...  7.34 us
    unnamed x10, local copies, waits for them, and re-layouts  4.55 us

profile of v1, /device:TPU:1, one launch (start us, length us, event | category | flops | bytes accessed | tf_op | source)
XLA Modules:
  0.0 65.8 jit_solution(13940409303159047281)
XLA Ops:
  0.0 0.0 copy-start
  0.0 1.4 %copy-done = bf16[48,16384]{1,0:T(8,128)(2,1)S(1)} copy-done((bf16[48,16384]{1,0:T(8,128)(2,1)S(1)}, bf16[48,16384]{1,0:T(8,128)(2,1)}, u32[]{:S(2)}) %copy-start) | copy-done | bytes 1572888
  1.4 0.0 copy-start.1
  1.4 1.1 %copy-done.1 = bf16[64,48,128]{2,1,0:T(8,128)(2,1)S(1)} copy-done((bf16[64,48,128]{2,1,0:T(8,128)(2,1)S(1)}, bf16[64,48,128]{2,1,0:T(8,128)(2,1)}, u32[]{:S(2)}) %copy-start.1) | copy-done | bytes 786456
  2.5 0.0 copy-start.2
  2.5 0.7 %copy-done.2 = f32[1,384]{1,0:T(1,128)S(1)} copy-done((f32[1,384]{1,0:T(1,128)S(1)}, f32[1,384]{1,0:T(1,128)}, u32[]{:S(2)}) %copy-start.2) | copy-done | bytes 1560
  3.2 0.0 copy-start.3
  3.2 0.7 %copy-done.3 = f32[1,384]{1,0:T(1,128)S(1)} copy-done((f32[1,384]{1,0:T(1,128)S(1)}, f32[1,384]{1,0:T(1,128)}, u32[]{:S(2)}) %copy-start.3) | copy-done | bytes 1560
  3.9 0.0 copy-start.4
  3.9 0.7 copy-done.4
  4.6 53.9 %partial_sums.1 = (f32[2,24,128]{2,1,0:T(8,128)S(1)}, bf16[3072,128]{1,0:T(8,128)(2,1)S(1)}) custom-call(bf16[3072,128]{1,0:T(8,128)(2,1)S(1)} %bitcast.2, bf16[128,16384]{1,0:T(8,128)(2,1)} %col_hbm.1, bf16[48,16384]{1,0:T(8,128)(2,1)S(1)} %copy-done, f32[1,384]{1,0:T(1,128)S(1)} %copy-done.2, f32[1,384]{1,0:T(1,128)S(1)} %copy-done.3, s32[128]{0:T(128)S(1)} %copy-done.4), custom_call_target="tpu_custom_call" | custom-call | tf_op jit(solution)/shard_map/partial_sums/pallas_call | solution.py:490
  58.4 7.3 %solve_apply.1 = bf16[3072,128]{1,0:T(8,128)(2,1)} custom-call(f32[2,24,128]{2,1,0:T(8,128)S(1)} %get-tuple-element.7.sums_ref, bf16[3072,128]{1,0:T(8,128)(2,1)S(1)} %get-tuple-element.8.et_ref), custom_call_target="tpu_custom_call" | custom-call | tf_op jit(solution)/shard_map/solve_apply/pallas_call | solution.py:540
Async XLA Ops:
  0.0 1.4 %copy-start = (bf16[48,16384]{1,0:T(8,128)(2,1)S(1)}, bf16[48,16384]{1,0:T(8,128)(2,1)}, u32[]{:S(2)}) copy-start(bf16[48,16384]{1,0:T(8,128)(2,1)} %row_hbm.1) | copy-start | bytes 4718596
  1.4 1.1 %copy-start.1 = (bf16[64,48,128]{2,1,0:T(8,128)(2,1)S(1)}, bf16[64,48,128]{2,1,0:T(8,128)(2,1)}, u32[]{:S(2)}) copy-start(bf16[64,48,128]{2,1,0:T(8,128)(2,1)} %param.6) | copy-start | bytes 2359300
  2.5 0.7 %copy-start.2 = (f32[1,384]{1,0:T(1,128)S(1)}, f32[1,384]{1,0:T(1,128)}, u32[]{:S(2)}) copy-start(f32[1,384]{1,0:T(1,128)} %obs_ref.1) | copy-start | bytes 4612
  3.2 0.7 %copy-start.3 = (f32[1,384]{1,0:T(1,128)S(1)}, f32[1,384]{1,0:T(1,128)}, u32[]{:S(2)}) copy-start(f32[1,384]{1,0:T(1,128)} %noise_ref.1) | copy-start | bytes 4612
  3.9 0.7 copy-start.4

commit v2 on v1

--- a/solution.py
+++ b/solution.py
@@ -35,10 +35,11 @@
 
 
 def partial_kernel(
-    e_hbm, col_hbm, row_hbm, obs_ref, noise_ref, owner_ref,
+    e_hbm, col_hbm, row_hbm, obs_hbm, noise_hbm, owner_hbm,
     sums_ref, et_hbm,
     e_v, ef, esend, erecv, lhs, col_v, row_v, csend, crecv, rhs, rowf, pa, pb, pc,
     ra1, ra2, ra3, rb1, rb2, rb3, rc1, rc2, rc3, slots, pack, got_core, got,
+    obs_ref, noise_ref, owner_ref, owner_row, small_sem,
     e_sem, et_sem, col_sem, row_sem,
     es_sem, er_sem, cs_sem, cr_sem,
     sa, sb, sc,
@@ -48,15 +49,19 @@
 ):
     y, x, z, k = here()
     sibling = device(y, x, z, 1 - k)
+    turn = 1 - 2 * k
 
     def zpeer(d):
-        return device(y, x, (z + d) % 4, k)
+        return device(y, x, (z + turn * d + 4) % 4, k)
 
     def xpeer(d):
-        return device(y, (x + d) % 4, z, k)
+        return device(y, (x + turn * d + 4) % 4, z, k)
 
     def ypeer(d):
-        return device((y + d) % 4, x, z, k)
+        return device((y + turn * d + 4) % 4, x, z, k)
+
+    def flat(d):
+        return device((y + d // 4) % 4, (x + d % 4) % 4, z, k)
 
     def remote(src, dst, send, recv, to):
         return pltpu.make_async_remote_copy(
@@ -72,7 +77,9 @@
 
     def span(core, s):
         dz, dx = 3 - s // 4, 3 - s % 4
-        first = ((core * 4 + (z + dz) % 4) * 4 + (x + dx) % 4) * WIDE
+        way = 1 - 2 * core
+        to_z, to_x = (z + way * dz + 4) % 4, (x + way * dx + 4) % 4
+        first = ((core * 4 + to_z) * 4 + to_x) * WIDE
         return pl.ds(pl.multiple_of(first, WIDE), WIDE)
 
     def load_col(which, s):
@@ -88,12 +95,20 @@
 
     load_e = pltpu.make_async_copy(e_hbm, e_v, e_sem)
     load_e.start()
+    load_small = [
+        pltpu.make_async_copy(src, dst, small_sem.at[i])
+        for i, (src, dst) in enumerate(
+            ((obs_hbm, obs_ref), (noise_hbm, noise_ref), (owner_hbm, owner_ref),
+             (owner_hbm, owner_row))
+        )
+    ]
+    for load in load_small:
+        load.start()
 
     barrier = pltpu.get_barrier_semaphore()
     pl.semaphore_signal(barrier, 1, device_id=sibling, device_id_type=MESH)
-    for d in (1, 2, 3):
-        for peer in (zpeer(d), xpeer(d), ypeer(d)):
-            pl.semaphore_signal(barrier, 1, device_id=peer, device_id_type=MESH)
+    for peer in [zpeer(d) for d in (1, 2, 3)] + [flat(d) for d in range(1, 16)]:
+        pl.semaphore_signal(barrier, 1, device_id=peer, device_id_type=MESH)
 
     def start_loads(s, carry):
         load_col(1, s).start()
@@ -105,6 +120,8 @@
 
     home = k * 64 + (y * 4 + x) * 4 + z
     pack[...] = jnp.zeros_like(pack)
+    for load in load_small:
+        load.wait()
     for i in range(CAP):
         pack[i:i + 1, :] = obs_ref[:, i * BLOCK:(i + 1) * BLOCK]
         pack[4 + i:5 + i, :] = noise_ref[:, i * BLOCK:(i + 1) * BLOCK]
@@ -113,7 +130,7 @@
     load_e.wait()
     ef[...] = e_v[...].astype(F32)
 
-    pl.semaphore_wait(barrier, 10)
+    pl.semaphore_wait(barrier, 19)
 
     quarter = MEMBERS * LROWS // 4
     for piece in range(4):
@@ -166,10 +183,10 @@
                 total += along[i * MEMBERS:(i + 1) * MEMBERS] * rowf[at:at + 1, :]
         for q in range(4):
             lanes = slice(q * BLOCK, (q + 1) * BLOCK)
-            turn = (q - y + 4) % 4
-            pa[s, turn] = total[0:24, lanes]
-            pb[s, turn] = total[24:48, lanes]
-            pc[s, turn] = total[48:64, lanes]
+            place = (turn * (q - y) + 4) % 4
+            pa[s, place] = total[0:24, lanes]
+            pb[s, place] = total[24:40, lanes]
+            pc[s, place] = total[40:64, lanes]
 
     def first_sends(w, j):
         s, dz, dx = 4 * w + j, 3 - w, 3 - j
@@ -322,7 +339,8 @@
             pl.when(s + AHEAD < STEPS)(functools.partial(send_col, s + AHEAD))
             compute(s)
             first_sends(w, j)
-            lagged((second_a, second_b, second_c), w, j, LAG2)
+            second_a(w, j)
+            lagged((second_b, second_c), w, j, LAG2)
             lagged((third_b, third_c), w, j, LAG3)
         pl.when(w == 0)(slots_x)
         pl.when(w == 1)(slots_y)
@@ -332,14 +350,12 @@
     lax.fori_loop(0, STEPS // 4, phase, 0)
 
     last = STEPS - 1
-    for s in range(STEPS - LAG2, last):
-        second_a(s // 4, s % 4)
-        second_b(s // 4, s % 4)
-        second_c(s // 4, s % 4)
-    for s in range(STEPS - LAG3, last):
-        third_b(s // 4, s % 4)
-        third_c(s // 4, s % 4)
-    second_a(3, 3)
+    third_b(2, 3)
+    second_c(3, 1)
+    third_c(3, 0)
+    third_c(3, 1)
+    second_c(3, 2)
+    third_c(3, 2)
     second_b(3, 3)
     third_a()
     second_c(3, 3)
@@ -348,19 +364,18 @@
 
     landed(slots.at[pl.ds(base_k, 64)], qo_k)
     me = ((k * 4 + z) * 4 + x) * 4 + y
-    owner = owner_ref[me]
-
-    def count(b, n):
-        return n + jnp.where(jnp.logical_and(owner_ref[b] == owner, b < me), 1, 0)
-
-    rank = lax.fori_loop(0, owner_ref.shape[0], count, jnp.int32(0))
+    owner = owner_ref[0, me]
+    owners = owner_row[...]
+    block_at = lax.broadcasted_iota(jnp.int32, (1, BLOCK), 1)
+    before = jnp.logical_and(owners == owner, block_at < me)
+    rank = jnp.sum(jnp.where(before, 1.0, 0.0), axis=1, keepdims=True)
     o_row, o_col = owner // 8, owner % 8
     found = slots[(o_col % 2) * 64 + o_row * 4 + o_col // 2]
     observed = jnp.where(
-        rank == 0, found[0:1], jnp.where(rank == 1, found[1:2], found[2:3])
+        rank < 0.5, found[0:1], jnp.where(rank < 1.5, found[1:2], found[2:3])
     )
     variance = jnp.where(
-        rank == 0, found[4:5], jnp.where(rank == 1, found[5:6], found[6:7])
+        rank < 0.5, found[4:5], jnp.where(rank < 1.5, found[5:6], found[6:7])
     )
     weight = 1.0 / variance
 
@@ -379,46 +394,46 @@
     mean = jnp.mean(predictions, axis=0, keepdims=True)
     anomalies = (predictions - mean) * (1.0 / ROOT)
     scaled = anomalies * weight
-    offset = jnp.where(
-        lax.broadcasted_iota(jnp.int32, (8, BLOCK), 0) == 0, observed - mean, 0.0
-    )
-    blank = jnp.zeros((8, BLOCK), F32)
-    left = jnp.concatenate([anomalies[0:16], anomalies[32:48], offset], axis=0)
-    right = jnp.concatenate([anomalies[16:32], anomalies[48:64], blank], axis=0)
-    none = jnp.zeros((MEMBERS, BLOCK), F32)
+    target = anomalies + (observed - mean)
+    blank = jnp.zeros((MEMBERS, BLOCK), F32)
     contract = (((1,), (1,)), ((), ()))
+    left = jnp.concatenate([scaled[0:16], scaled[32:48]], axis=0)
+    right = jnp.concatenate([scaled[16:32], scaled[48:64]], axis=0)
     packed = lax.dot_general(
-        left, jnp.concatenate([scaled, none], axis=0), contract,
+        left, jnp.concatenate([target, blank], axis=0), contract,
         precision=lax.Precision.HIGHEST, preferred_element_type=F32,
     ) + lax.dot_general(
-        right, jnp.concatenate([none, scaled], axis=0), contract,
+        right, jnp.concatenate([blank, target], axis=0), contract,
         precision=lax.Precision.HIGHEST, preferred_element_type=F32,
     )
-    got[0, 0, 0:16] = packed[0:16]
-    got[0, 0, 16:24] = packed[32:40]
-    got[0, 1, 0:16] = packed[16:32]
-    got[0, 1, 16:24] = jnp.zeros((8, BLOCK), F32)
+    got[0, 0] = packed[0:16]
+    got[0, 1] = packed[16:32]
 
     remote(got.at[0, 1 - k], got_core.at[0], st.at[0], qt.at[0], sibling).start()
     landed(got_core.at[0], qt.at[0])
     got[1, 0] = got[0, k] + got_core[0]
-    for stage, peers in enumerate((zpeer, xpeer, ypeer)):
-        for d in (1, 2, 3):
-            remote(
-                got.at[1 + stage, 0], got_core.at[1 + 3 * stage + d - 1],
-                st.at[1 + 3 * stage + d - 1], qt.at[1 + 3 * stage + d - 1], peers(d),
-            ).start()
-        for d in (1, 2, 3):
-            landed(got_core.at[1 + 3 * stage + d - 1], qt.at[1 + 3 * stage + d - 1])
-        first = 1 + 3 * stage
-        total = got[1 + stage, 0] + (
-            got_core[first] + (got_core[first + 1] + got_core[first + 2])
-        )
-        got[2 + stage, 0] = total
-    remote(got.at[4, 0], got_core.at[10], st.at[10], qt.at[10], sibling).start()
-    sums_ref[k] = got[4, 0]
-    landed(got_core.at[10], qt.at[10])
-    sums_ref[1 - k] = got_core[10]
+    for d in (1, 2, 3):
+        remote(
+            got.at[1, 0], got_core.at[d], st.at[d], qt.at[d], zpeer(d)
+        ).start()
+    for d in (1, 2, 3):
+        landed(got_core.at[d], qt.at[d])
+    got[2, 0] = got[1, 0] + (got_core[1] + (got_core[2] + got_core[3]))
+    for d in range(1, 16):
+        remote(
+            got.at[2, 0], got_core.at[3 + d], st.at[3 + d], qt.at[3 + d], flat(d)
+        ).start()
+    total = got[2, 0]
+    for d in range(1, 16):
+        landed(got_core.at[3 + d], qt.at[3 + d])
+        total += got_core[3 + d]
+    got[3, 0] = total
+    end = 19
+    whole = 3
+    remote(got.at[whole, 0], got_core.at[end], st.at[end], qt.at[end], sibling).start()
+    sums_ref[k] = got[whole, 0]
+    landed(got_core.at[end], qt.at[end])
+    sums_ref[1 - k] = got_core[end]
 
     save_et.wait()
     sent(esend, es_sem)
@@ -433,28 +448,82 @@
     sent(pc.at[pl.ds(0, 12), 0], sc.at[1])
     sent(pc.at[0, pl.ds(0, 3)], sc.at[2])
     sent(slots.at[pl.ds(0, 3 + 12 + 48 + 64)], so)
-    for i in range(11):
+    for i in range(20):
         sent(got_core.at[0], st.at[i])
 
 
-def apply_kernel(sums_ref, et_ref, out_ref, full):
-    low = sums_ref[0, 0:16]
-    high = sums_ref[1, 0:16]
-    spread = jnp.concatenate(
+def lane(panel, at):
+    return jnp.broadcast_to(panel[:, at:at + 1], panel.shape)
+
+
+def sub(panel, at):
+    return jnp.broadcast_to(panel[at:at + 1], panel.shape)
+
+
+def pivot_four(panel, column, t):
+    at = lax.broadcasted_iota(jnp.int32, panel.shape, 0)
+    c = [lane(panel, column + t + i) for i in range(4)]
+    r = [sub(panel, t + i) for i in range(4)]
+    a, q, d = sub(c[0], t), sub(c[0], t + 1), sub(c[1], t + 1)
+    e00, e01, e10, e11 = (
+        sub(c[0], t + 2), sub(c[1], t + 2), sub(c[0], t + 3), sub(c[1], t + 3)
+    )
+    f, g, h = sub(c[2], t + 2), sub(c[2], t + 3), sub(c[3], t + 3)
+    inv = 1.0 / (a * d - q * q)
+    w00, w01 = (e00 * d - e01 * q) * inv, (e01 * a - e00 * q) * inv
+    w10, w11 = (e10 * d - e11 * q) * inv, (e11 * a - e10 * q) * inv
+    f = f - (w00 * e00 + w01 * e01)
+    g = g - (w00 * e10 + w01 * e11)
+    h = h - (w10 * e10 + w11 * e11)
+    rest = 1.0 / (f * h - g * g)
+    u = r[2] - (w00 * r[0] + w01 * r[1])
+    v = r[3] - (w10 * r[0] + w11 * r[1])
+    n2, n3 = (h * u - g * v) * rest, (f * v - g * u) * rest
+    n0 = (d * r[0] - q * r[1]) * inv - (w00 * n2 + w10 * n3)
+    n1 = (a * r[1] - q * r[0]) * inv - (w01 * n2 + w11 * n3)
+    new = panel - ((c[0] * n0 + c[1] * n1) + (c[2] * n2 + c[3] * n3))
+    for i, row in enumerate((n0, n1, n2, n3)):
+        new = jnp.where(at == t + i, row, new)
+    return new
+
+
+def eliminate(grid):
+    panels = [grid[8 * i:8 * i + 8] for i in range(8)]
+    for b in range(8):
+        columns = [
+            [lane(panels[i], 8 * b + t) for t in range(8)] if i != b else None
+            for i in range(8)
+        ]
+        done = pivot_four(pivot_four(panels[b], 8 * b, 0), 8 * b, 4)
+        rows = [sub(done, t) for t in range(8)]
+        for i in range(8):
+            if i != b:
+                m = [columns[i][t] * rows[t] for t in range(8)]
+                panels[i] = panels[i] - (
+                    ((m[0] + m[1]) + (m[2] + m[3])) + ((m[4] + m[5]) + (m[6] + m[7]))
+                )
+        panels[b] = done
+    return jnp.concatenate(panels, axis=0)
+
+
+def apply_kernel(sums_ref, et_hbm, out_ref, full, et_ref, et_sem):
+    load = pltpu.make_async_copy(et_hbm, et_ref, et_sem)
+    load.start()
+    low, high = sums_ref[0], sums_ref[1]
+    both = jnp.concatenate(
         [low, pltpu.roll(low, 64, 1), high, pltpu.roll(high, 64, 1)], axis=0
     )
-    r_row = sums_ref[0, 16:17] + sums_ref[1, 16:17]
     row_at = lax.broadcasted_iota(jnp.int32, (MEMBERS, 2 * MEMBERS), 0)
     lane_at = lax.broadcasted_iota(jnp.int32, (MEMBERS, 2 * MEMBERS), 1)
     left = lane_at < MEMBERS
+    r_col = jnp.sum(jnp.where(left, both, 0.0), axis=1, keepdims=True) * (1.0 / MEMBERS)
     eye = jnp.where(row_at == lane_at, 1.0, 0.0)
-    grid = jnp.where(left, spread + eye, jnp.where(lane_at - MEMBERS == row_at, 1.0, 0.0))
-    for p in range(MEMBERS):
-        pivot_row = grid[p:p + 1, :]
-        scaled = pivot_row / pivot_row[:, p:p + 1]
-        grid = jnp.where(row_at == p, scaled, grid - grid[:, p:p + 1] * scaled)
+    grid = eliminate(
+        jnp.where(
+            left, (both - r_col) + eye, jnp.where(lane_at - MEMBERS == row_at, 1.0, 0.0)
+        )
+    )
     inverse = jnp.where(left, pltpu.roll(grid, 64, 1), 0.0)
-    r_col = jnp.sum(jnp.where(row_at == lane_at, r_row, 0.0), axis=1, keepdims=True)
     shift = jnp.sum(inverse * r_col, axis=0, keepdims=True)
     gain_t = jnp.where(left, shift - ROOT * (eye - inverse), 0.0)
     centre = jnp.sum(gain_t, axis=1, keepdims=True) * (1.0 / MEMBERS)
@@ -464,8 +533,9 @@
     three = moves - one - two
     factors = jnp.concatenate(
         [(one + pltpu.roll(two, 64, 1)).astype(BF16), three.astype(BF16)], axis=1
-    )[:, 0:2 * BLOCK]
+    )
     zero = jnp.zeros((MEMBERS, 2 * BLOCK), BF16)
+    load.wait()
     for g in range(LROWS // 2):
         at = 2 * g * MEMBERS
         pair = jnp.concatenate(
@@ -484,17 +554,16 @@
     field = ensemble.reshape(MEMBERS * LROWS, LCOLS)
     hbm = pl.BlockSpec(memory_space=pltpu.HBM)
     vmem = pl.BlockSpec(memory_space=pltpu.VMEM)
-    smem = pl.BlockSpec(memory_space=pltpu.SMEM)
     dma = pltpu.SemaphoreType.DMA
     size = MEMBERS * LROWS
     sums, field_t = pl.pallas_call(
         partial_kernel,
         name="partial_sums",
         out_shape=(
-            jax.ShapeDtypeStruct((2, 24, BLOCK), F32),
+            jax.ShapeDtypeStruct((2, 16, BLOCK), F32),
             jax.ShapeDtypeStruct((size, LCOLS), BF16),
         ),
-        in_specs=[hbm, hbm, hbm, vmem, vmem, smem],
+        in_specs=[hbm] * 6,
         out_specs=(vmem, hbm),
         scratch_shapes=[
             pltpu.VMEM((size, LCOLS), BF16),
@@ -509,21 +578,26 @@
             pltpu.VMEM((2 * LCOLS, WIDE), BF16),
             pltpu.VMEM((LROWS, WIDE), F32),
             pltpu.VMEM((STEPS, 4, 24, BLOCK), F32),
+            pltpu.VMEM((STEPS, 4, 16, BLOCK), F32),
             pltpu.VMEM((STEPS, 4, 24, BLOCK), F32),
-            pltpu.VMEM((STEPS, 4, 16, BLOCK), F32),
             pltpu.VMEM((3, 4, 4, 24, BLOCK), F32),
             pltpu.VMEM((3, 4, 24, BLOCK), F32),
             pltpu.VMEM((3, 24, BLOCK), F32),
-            pltpu.VMEM((4, 3, 4, 24, BLOCK), F32),
-            pltpu.VMEM((4, 3, 24, BLOCK), F32),
+            pltpu.VMEM((4, 3, 4, 16, BLOCK), F32),
+            pltpu.VMEM((4, 3, 16, BLOCK), F32),
+            pltpu.VMEM((3, 16, BLOCK), F32),
+            pltpu.VMEM((STEPS, 3, 24, BLOCK), F32),
+            pltpu.VMEM((3, 4, 24, BLOCK), F32),
             pltpu.VMEM((3, 24, BLOCK), F32),
-            pltpu.VMEM((STEPS, 3, 16, BLOCK), F32),
-            pltpu.VMEM((3, 4, 16, BLOCK), F32),
-            pltpu.VMEM((3, 16, BLOCK), F32),
             pltpu.VMEM((128, 8, BLOCK), F32),
             pltpu.VMEM((8, BLOCK), F32),
-            pltpu.VMEM((11, 24, BLOCK), F32),
-            pltpu.VMEM((5, 2, 24, BLOCK), F32),
+            pltpu.VMEM((20, 16, BLOCK), F32),
+            pltpu.VMEM((5, 2, 16, BLOCK), F32),
+            pltpu.VMEM((1, CAP * BLOCK), F32),
+            pltpu.VMEM((1, CAP * BLOCK), F32),
+            pltpu.SMEM((1, BLOCK), jnp.int32),
+            pltpu.VMEM((1, BLOCK), jnp.int32),
+            dma((4,)),
             dma, dma, dma((2, STEPS)), dma((STEPS,)),
             dma, dma((4,)), dma, dma((STEPS,)),
             dma((3,)), dma((3,)), dma((3,)),
@@ -531,20 +605,22 @@
             dma((4, 3)), dma((4, 3)), dma((3,)),
             dma((STEPS, 3)), dma((3, 4)), dma((3,)),
             dma, dma((3,)), dma((3,)), dma((3,)), dma,
-            dma((11,)), dma((11,)),
+            dma((20,)), dma((20,)),
         ],
         compiler_params=pltpu.CompilerParams(
-            collective_id=0, has_side_effects=True, vmem_limit_bytes=48 << 20
+            collective_id=0, has_side_effects=True, vmem_limit_bytes=62 << 20
         ),
-    )(field, col_profile, row_profile, obs_owned, noise_owned, block_owner)
+    )(field, col_profile, row_profile, obs_owned, noise_owned, block_owner.reshape(1, -1))
     moved = pl.pallas_call(
         apply_kernel,
         name="solve_apply",
         out_shape=jax.ShapeDtypeStruct((size, LCOLS), BF16),
-        in_specs=[vmem, vmem],
+        in_specs=[vmem, hbm],
         out_specs=vmem,
-        scratch_shapes=[pltpu.VMEM((size, LCOLS), F32)],
-        compiler_params=pltpu.CompilerParams(vmem_limit_bytes=32 << 20),
+        scratch_shapes=[
+            pltpu.VMEM((size, LCOLS), F32), pltpu.VMEM((size, LCOLS), BF16), dma
+        ],
+        compiler_params=pltpu.CompilerParams(vmem_limit_bytes=62 << 20),
     )(sums, field_t)
     return moved.reshape(ensemble.shape)
 

time: 66 us -> 58.4 us (0.88)
  local copies, waits for them, and re-layouts: 4.55 us -> 0 us
  Pallas kernels: 61.2 us -> 58.2 us
    unnamed x10 -> x0, local copies, waits for them, and re-layouts: 4.55 us -> none
    pallas_call x1, Pallas kernels: 53.9 us -> 51.9 us  [on_device(): pl.pallas_call(partial_kernel, name='partial_sums', out_shape=(jax.ShapeD...]
    pallas_call x1, Pallas kernels: 7.34 us -> 6.35 us  [on_device(): pl.pallas_call(apply_kernel, name='solve_apply', out_shape=jax.ShapeDtype...]
where the time goes in v2:
time: 58.4 us; the launch traced here: 58.2 us
  Pallas kernels  58.2 us (100%)
    pallas_call x1, Pallas kernels, on_device(): pl.pallas_call(partial_kernel, name='partial_sums', out_shape=(jax.ShapeD...  51.9 us
    pallas_call x1, Pallas kernels, on_device(): pl.pallas_call(apply_kernel, name='solve_apply', out_shape=jax.ShapeDtype...  6.35 us

profile of v2, /device:TPU:1, one launch (start us, length us, event | category | flops | bytes accessed | tf_op | source)
XLA Modules:
  0.0 58.2 jit_solution(17850281801852849954)
XLA Ops:
  0.0 51.9 %partial_sums.1 = (f32[2,16,128]{2,1,0:T(8,128)}, bf16[3072,128]{1,0:T(8,128)(2,1)}) custom-call(bf16[3072,128]{1,0:T(8,128)(2,1)} %bitcast.3, bf16[128,16384]{1,0:T(8,128)(2,1)} %col_hbm.1, bf16[48,16384]{1,0:T(8,128)(2,1)} %row_hbm.1, f32[1,384]{1,0:T(1,128)} %obs_hbm.1, f32[1,384]{1,0:T(1,128)} %noise_hbm.1, s32[1,128]{1,0:T(1,128)} %bitcast.4), custom_call_target="tpu_custom_call" | custom-call | tf_op jit(solution)/shard_map/partial_sums/pallas_call | solution.py:559
  51.9 6.3 %solve_apply.1 = bf16[3072,128]{1,0:T(8,128)(2,1)} custom-call(f32[2,16,128]{2,1,0:T(8,128)} %get-tuple-element.7.sums_ref, bf16[3072,128]{1,0:T(8,128)(2,1)} %get-tuple-element.8.et_hbm), custom_call_target="tpu_custom_call" | custom-call | tf_op jit(solution)/shard_map/solve_apply/pallas_call | solution.py:614

commit v3 on v2

--- a/solution.py
+++ b/solution.py
@@ -93,8 +93,14 @@
             row_hbm.at[:, span(k, s)], row_v.at[s], row_sem.at[s]
         )
 
-    load_e = pltpu.make_async_copy(e_hbm, e_v, e_sem)
-    load_e.start()
+    load_e = [
+        pltpu.make_async_copy(
+            e_hbm.at[:, pl.ds(16 * i, 16), :], e_v.at[i], e_sem.at[i]
+        )
+        for i in range(3)
+    ]
+    for load in load_e:
+        load.start()
     load_small = [
         pltpu.make_async_copy(src, dst, small_sem.at[i])
         for i, (src, dst) in enumerate(
@@ -118,7 +124,7 @@
 
     lax.fori_loop(0, STEPS, start_loads, 0)
 
-    home = k * 64 + (y * 4 + x) * 4 + z
+    home = k * 64 + (x * 4 + y) * 4 + z
     pack[...] = jnp.zeros_like(pack)
     for load in load_small:
         load.wait()
@@ -127,21 +133,23 @@
         pack[4 + i:5 + i, :] = noise_ref[:, i * BLOCK:(i + 1) * BLOCK]
     slots[home] = pack[...]
 
-    load_e.wait()
-    ef[...] = e_v[...].astype(F32)
-
     pl.semaphore_wait(barrier, 19)
 
-    quarter = MEMBERS * LROWS // 4
-    for piece in range(4):
-        for i in range(12):
-            at = piece * 12 + i
-            plane = ef[pl.ds(at, MEMBERS, stride=LROWS), :]
+    for d in (1, 2, 3):
+        remote(slots.at[home], slots.at[home], so, qo_z.at[d - 1], zpeer(d)).start()
+
+    third = MEMBERS * LROWS // 3
+    for piece in range(3):
+        load_e[piece].wait()
+        ef[piece] = e_v[piece].astype(F32).reshape(third, LCOLS)
+        for i in range(16):
+            at = piece * 16 + i
+            plane = ef[piece, pl.ds(i, MEMBERS, stride=16), :]
             esend[at * MEMBERS:(at + 1) * MEMBERS, :] = plane
             lhs[at * MEMBERS:(at + 1) * MEMBERS, 0:LCOLS] = plane.astype(BF16)
-        part_rows = pl.ds(piece * quarter, quarter)
+        rows = pl.ds(piece * third, third)
         remote(
-            esend.at[part_rows], erecv.at[part_rows], es_sem, er_sem.at[piece], sibling
+            esend.at[rows], erecv.at[rows], es_sem, er_sem.at[piece], sibling
         ).start()
 
     def send_col(s):
@@ -152,14 +160,10 @@
     for s in range(AHEAD):
         send_col(s)
 
-    for d in (1, 2, 3):
-        remote(slots.at[home], slots.at[home], so, qo_z.at[d - 1], zpeer(d)).start()
-
-    for piece in range(4):
-        part_rows = pl.ds(piece * quarter, quarter)
-        landed(erecv.at[part_rows], er_sem.at[piece])
-        lhs[piece * quarter:(piece + 1) * quarter, LCOLS:2 * LCOLS] = (
-            erecv[piece * quarter:(piece + 1) * quarter, :].astype(BF16)
+    for piece in range(3):
+        landed(erecv.at[pl.ds(piece * third, third)], er_sem.at[piece])
+        lhs[piece * third:(piece + 1) * third, LCOLS:2 * LCOLS] = (
+            erecv[piece * third:(piece + 1) * third, :].astype(BF16)
         )
     save_et = pltpu.make_async_copy(lhs.at[:, pl.ds(0, LCOLS)], et_hbm, et_sem)
     save_et.start()
@@ -296,27 +300,27 @@
                     sc.at[2], qc3.at[dx - 1], xpeer(dx),
                 ).start()
 
-    base_x = k * 64 + (y * 4 + x) * 4
-    base_y = k * 64 + y * 16
+    base_y = k * 64 + (x * 4 + y) * 4
+    base_x = k * 64 + x * 16
     base_k = k * 64
+
+    def slots_y():
+        for d in (1, 2, 3):
+            landed(slots.at[home], qo_z.at[d - 1])
+        mine = slots.at[pl.ds(base_y, 4)]
+        for d in (1, 2, 3):
+            remote(mine, mine, so, qo_y.at[d - 1], ypeer(d)).start()
 
     def slots_x():
         for d in (1, 2, 3):
-            landed(slots.at[home], qo_z.at[d - 1])
-        mine = slots.at[pl.ds(base_x, 4)]
+            landed(slots.at[pl.ds(base_y, 4)], qo_y.at[d - 1])
+        mine = slots.at[pl.ds(base_x, 16)]
         for d in (1, 2, 3):
             remote(mine, mine, so, qo_x.at[d - 1], xpeer(d)).start()
 
-    def slots_y():
-        for d in (1, 2, 3):
-            landed(slots.at[pl.ds(base_x, 4)], qo_x.at[d - 1])
-        mine = slots.at[pl.ds(base_y, 16)]
-        for d in (1, 2, 3):
-            remote(mine, mine, so, qo_y.at[d - 1], ypeer(d)).start()
-
     def slots_k():
         for d in (1, 2, 3):
-            landed(slots.at[pl.ds(base_y, 16)], qo_y.at[d - 1])
+            landed(slots.at[pl.ds(base_x, 16)], qo_x.at[d - 1])
         mine = slots.at[pl.ds(base_k, 64)]
         remote(mine, mine, so, qo_k, sibling).start()
 
@@ -340,24 +344,24 @@
             compute(s)
             first_sends(w, j)
             second_a(w, j)
-            lagged((second_b, second_c), w, j, LAG2)
-            lagged((third_b, third_c), w, j, LAG3)
+            lagged((second_b,), w, j, 2)
+            lagged((second_c, third_c), w, j, 3)
+            lagged((third_b,), w, j, 5)
         pl.when(w == 0)(slots_x)
-        pl.when(w == 1)(slots_y)
-        pl.when(w == 2)(slots_k)
+        pl.when(w == 1)(slots_k)
         return carry
 
+    slots_y()
     lax.fori_loop(0, STEPS // 4, phase, 0)
 
     last = STEPS - 1
+    second_c(3, 1)
+    third_c(3, 1)
     third_b(2, 3)
-    second_c(3, 1)
-    third_c(3, 0)
-    third_c(3, 1)
+    second_b(3, 3)
+    third_a()
     second_c(3, 2)
     third_c(3, 2)
-    second_b(3, 3)
-    third_a()
     second_c(3, 3)
     third_c(3, 3)
     third_b(3, 3)
@@ -370,7 +374,9 @@
     before = jnp.logical_and(owners == owner, block_at < me)
     rank = jnp.sum(jnp.where(before, 1.0, 0.0), axis=1, keepdims=True)
     o_row, o_col = owner // 8, owner % 8
-    found = slots[(o_col % 2) * 64 + o_row * 4 + o_col // 2]
+    found = slots[
+        (o_col % 2) * 64 + (o_row % 4) * 16 + (o_row // 4) * 4 + o_col // 2
+    ]
     observed = jnp.where(
         rank < 0.5, found[0:1], jnp.where(rank < 1.5, found[1:2], found[2:3])
     )
@@ -551,7 +557,6 @@
 
 
 def on_device(ensemble, row_profile, col_profile, obs_owned, noise_owned, block_owner):
-    field = ensemble.reshape(MEMBERS * LROWS, LCOLS)
     hbm = pl.BlockSpec(memory_space=pltpu.HBM)
     vmem = pl.BlockSpec(memory_space=pltpu.VMEM)
     dma = pltpu.SemaphoreType.DMA
@@ -566,8 +571,8 @@
         in_specs=[hbm] * 6,
         out_specs=(vmem, hbm),
         scratch_shapes=[
-            pltpu.VMEM((size, LCOLS), BF16),
-            pltpu.VMEM((size, LCOLS), F32),
+            pltpu.VMEM((3, MEMBERS, 16, LCOLS), BF16),
+            pltpu.VMEM((3, size // 3, LCOLS), F32),
             pltpu.VMEM((size, LCOLS), F32),
             pltpu.VMEM((size, LCOLS), F32),
             pltpu.VMEM((size, 2 * LCOLS), BF16),
@@ -598,8 +603,8 @@
             pltpu.SMEM((1, BLOCK), jnp.int32),
             pltpu.VMEM((1, BLOCK), jnp.int32),
             dma((4,)),
-            dma, dma, dma((2, STEPS)), dma((STEPS,)),
-            dma, dma((4,)), dma, dma((STEPS,)),
+            dma((3,)), dma, dma((2, STEPS)), dma((STEPS,)),
+            dma, dma((3,)), dma, dma((STEPS,)),
             dma((3,)), dma((3,)), dma((3,)),
             dma((3, 4)), dma((3,)), dma((3,)),
             dma((4, 3)), dma((4, 3)), dma((3,)),
@@ -610,7 +615,7 @@
         compiler_params=pltpu.CompilerParams(
             collective_id=0, has_side_effects=True, vmem_limit_bytes=62 << 20
         ),
-    )(field, col_profile, row_profile, obs_owned, noise_owned, block_owner.reshape(1, -1))
+    )(ensemble, col_profile, row_profile, obs_owned, noise_owned, block_owner.reshape(1, -1))
     moved = pl.pallas_call(
         apply_kernel,
         name="solve_apply",

time: 58.4 us -> 57.9 us (level)
  no operation moved by 1% of the time
where the time goes in v3:
time: 57.9 us; the launch traced here: 57.7 us
  Pallas kernels  57.7 us (100%)
    pallas_call x1, Pallas kernels, on_device(): pl.pallas_call(partial_kernel, name='partial_sums', out_shape=(jax.ShapeD...  51.3 us
    pallas_call x1, Pallas kernels, on_device(): pl.pallas_call(apply_kernel, name='solve_apply', out_shape=jax.ShapeDtype...  6.35 us

profile of v3, /device:TPU:1, one launch (start us, length us, event | category | flops | bytes accessed | tf_op | source)
XLA Modules:
  0.0 57.7 jit_solution(5692014759595842672)
XLA Ops:
  0.0 51.3 %partial_sums.1 = (f32[2,16,128]{2,1,0:T(8,128)}, bf16[3072,128]{1,0:T(8,128)(2,1)}) custom-call(bf16[64,48,128]{2,1,0:T(8,128)(2,1)} %e_hbm.1, bf16[128,16384]{1,0:T(8,128)(2,1)} %col_hbm.1, bf16[48,16384]{1,0:T(8,128)(2,1)} %row_hbm.1, f32[1,384]{1,0:T(1,128)} %obs_hbm.1, f32[1,384]{1,0:T(1,128)} %noise_hbm.1, s32[1,128]{1,0:T(1,128)} %bitcast.2), custom_call_target="tpu_custom_call" | custom-call | tf_op jit(solution)/shard_map/partial_sums/pallas_call | solution.py:564
  51.4 6.3 %solve_apply.1 = bf16[3072,128]{1,0:T(8,128)(2,1)} custom-call(f32[2,16,128]{2,1,0:T(8,128)} %get-tuple-element.7.sums_ref, bf16[3072,128]{1,0:T(8,128)(2,1)} %get-tuple-element.8.et_hbm), custom_call_target="tpu_custom_call" | custom-call | tf_op jit(solution)/shard_map/solve_apply/pallas_call | solution.py:619

commit v4 on v3

--- a/solution.py
+++ b/solution.py
@@ -208,7 +208,7 @@
                 sb.at[0], qb1.at[w, dx - 1], xpeer(dx),
             ).start()
 
-        for d in (1, 2, 3):
+        for d in (2, 1, 3):
             remote(
                 pc.at[s, d], rc1.at[s, d - 1],
                 sc.at[0], qc1.at[s, d - 1], ypeer(d),
@@ -238,7 +238,7 @@
             for p in range(3):
                 landed(rb1.at[w, p], qb1.at[w, p])
             pb[s] = pb[s] + (rb1[w, 0] + (rb1[w, 1] + rb1[w, 2]))
-            for d in (1, 2, 3):
+            for d in (2, 1, 3):
                 remote(
                     pb.at[s, d], rb2.at[w, d - 1],
                     sb.at[1], qb2.at[w, d - 1], ypeer(d),
@@ -262,7 +262,7 @@
         for p in range(3):
             landed(ra2.at[p], qa2.at[p])
         pa[s] = pa[s] + (ra2[0] + (ra2[1] + ra2[2]))
-        for d in (1, 2, 3):
+        for d in (2, 1, 3):
             remote(
                 pa.at[s, d], ra3.at[d - 1],
                 sa.at[2], qa3.at[d - 1], ypeer(d),
@@ -418,14 +418,14 @@
     remote(got.at[0, 1 - k], got_core.at[0], st.at[0], qt.at[0], sibling).start()
     landed(got_core.at[0], qt.at[0])
     got[1, 0] = got[0, k] + got_core[0]
-    for d in (1, 2, 3):
+    for d in (2, 1, 3):
         remote(
             got.at[1, 0], got_core.at[d], st.at[d], qt.at[d], zpeer(d)
         ).start()
     for d in (1, 2, 3):
         landed(got_core.at[d], qt.at[d])
     got[2, 0] = got[1, 0] + (got_core[1] + (got_core[2] + got_core[3]))
-    for d in range(1, 16):
+    for d in (10, 9, 11, 6, 14, 5, 7, 13, 15, 8, 2, 4, 12, 1, 3):
         remote(
             got.at[2, 0], got_core.at[3 + d], st.at[3 + d], qt.at[3 + d], flat(d)
         ).start()

time: 57.9 us -> 57.4 us (level)
  no operation moved by 1% of the time
where the time goes in v4:
time: 57.4 us; the launch traced here: 57.2 us
  Pallas kernels  57.2 us (100%)
    pallas_call x1, Pallas kernels, on_device(): pl.pallas_call(partial_kernel, name='partial_sums', out_shape=(jax.ShapeD...  50.9 us
    pallas_call x1, Pallas kernels, on_device(): pl.pallas_call(apply_kernel, name='solve_apply', out_shape=jax.ShapeDtype...  6.35 us

profile of v4, /device:TPU:1, one launch (start us, length us, event | category | flops | bytes accessed | tf_op | source)
XLA Modules:
  0.0 57.2 jit_solution(3914817317269463574)
XLA Ops:
  0.0 50.9 %partial_sums.1 = (f32[2,16,128]{2,1,0:T(8,128)}, bf16[3072,128]{1,0:T(8,128)(2,1)}) custom-call(bf16[64,48,128]{2,1,0:T(8,128)(2,1)} %e_hbm.1, bf16[128,16384]{1,0:T(8,128)(2,1)} %col_hbm.1, bf16[48,16384]{1,0:T(8,128)(2,1)} %row_hbm.1, f32[1,384]{1,0:T(1,128)} %obs_hbm.1, f32[1,384]{1,0:T(1,128)} %noise_hbm.1, s32[1,128]{1,0:T(1,128)} %bitcast.2), custom_call_target="tpu_custom_call" | custom-call | tf_op jit(solution)/shard_map/partial_sums/pallas_call | solution.py:564
  50.9 6.3 %solve_apply.1 = bf16[3072,128]{1,0:T(8,128)(2,1)} custom-call(f32[2,16,128]{2,1,0:T(8,128)} %get-tuple-element.7.sums_ref, bf16[3072,128]{1,0:T(8,128)(2,1)} %get-tuple-element.8.et_hbm), custom_call_target="tpu_custom_call" | custom-call | tf_op jit(solution)/shard_map/solve_apply/pallas_call | solution.py:619

commit v5 on v4

--- a/solution.py
+++ b/solution.py
@@ -113,7 +113,9 @@
 
     barrier = pltpu.get_barrier_semaphore()
     pl.semaphore_signal(barrier, 1, device_id=sibling, device_id_type=MESH)
-    for peer in [zpeer(d) for d in (1, 2, 3)] + [flat(d) for d in range(1, 16)]:
+    for peer in [
+        flat(d) for d in (10, 9, 11, 6, 14, 5, 7, 13, 15, 8, 2, 4, 12, 1, 3)
+    ] + [zpeer(d) for d in (2, 1, 3)]:
         pl.semaphore_signal(barrier, 1, device_id=peer, device_id_type=MESH)
 
     def start_loads(s, carry):

time: 57.4 us -> 57.3 us (level)
  no operation moved by 1% of the time
where the time goes in v5:
time: 57.3 us; the launch traced here: 57.1 us
  Pallas kernels  57.1 us (100%)
    pallas_call x1, Pallas kernels, on_device(): pl.pallas_call(partial_kernel, name='partial_sums', out_shape=(jax.ShapeD...  50.7 us
    pallas_call x1, Pallas kernels, on_device(): pl.pallas_call(apply_kernel, name='solve_apply', out_shape=jax.ShapeDtype...  6.35 us

profile of v5, /device:TPU:1, one launch (start us, length us, event | category | flops | bytes accessed | tf_op | source)
XLA Modules:
  0.0 57.1 jit_solution(8844429258639168462)
XLA Ops:
  0.0 50.7 %partial_sums.1 = (f32[2,16,128]{2,1,0:T(8,128)}, bf16[3072,128]{1,0:T(8,128)(2,1)}) custom-call(bf16[64,48,128]{2,1,0:T(8,128)(2,1)} %e_hbm.1, bf16[128,16384]{1,0:T(8,128)(2,1)} %col_hbm.1, bf16[48,16384]{1,0:T(8,128)(2,1)} %row_hbm.1, f32[1,384]{1,0:T(1,128)} %obs_hbm.1, f32[1,384]{1,0:T(1,128)} %noise_hbm.1, s32[1,128]{1,0:T(1,128)} %bitcast.2), custom_call_target="tpu_custom_call" | custom-call | tf_op jit(solution)/shard_map/partial_sums/pallas_call | solution.py:566
  50.7 6.3 %solve_apply.1 = bf16[3072,128]{1,0:T(8,128)(2,1)} custom-call(f32[2,16,128]{2,1,0:T(8,128)} %get-tuple-element.7.sums_ref, bf16[3072,128]{1,0:T(8,128)(2,1)} %get-tuple-element.8.et_hbm), custom_call_target="tpu_custom_call" | custom-call | tf_op jit(solution)/shard_map/solve_apply/pallas_call | solution.py:621
